TPU v7x, 128 devices: a whole 4x4x4 slice. The times are simulated.
128 devices in a mesh: group: 8 (over y_hi, x), fsdp: 16 (over z, y_lo, core).
Axes of the slice: x: 4, y: 4 (y_hi: 2, y_lo: 2; y = y_hi * 2 + y_lo), z: 4, core: 2. Of those that a mesh axis runs over, the one named last changes fastest.
Arguments:
- tokens_in: bfloat16 [131072, 2048], P(('group', 'fsdp')), may hold values from -6 to 6
- out_grad: bfloat16 [131072, 2048], P(('group', 'fsdp')), may hold values from -0.59765625 to 0.59765625
- w_in: bfloat16 [8, 2048, 8192], P('group', None, 'fsdp'), may hold values from -0.125 to 0.125
- w_out: bfloat16 [8, 8192, 2048], P('group', 'fsdp'), may hold values from -0.0625 to 0.0625
- chosen: int32 [128, 8, 16], P(('group', 'fsdp')), may hold values from 0 to 1023, as said below
- counts: int32 [128, 8], P(('group', 'fsdp')), may hold values from 1 to 16, as said below
- gates: float32 [128, 8, 16], P(('group', 'fsdp')), may hold values from 0.05 to 1
Outputs:
- grad_in: bfloat16 [131072, 2048], P(('group', 'fsdp'))
- grad_w_in: float32 [8, 2048, 8192], P('group', None, 'fsdp')
- grad_w_out: float32 [8, 8192, 2048], P('group', 'fsdp')
Inputs may be any that keep to these rules, and one draw needn't show every extreme that they name: `chosen`: the 16 slots of one image and one expert name distinct positions. `counts`: each image fills all 16 slots of at least one expert.
All inputs are finite; a program needn't handle non-finite values.
Results may differ from a plain program's by a relative error of at most 0.0057.
Values may be sent and summed in bfloat16 or wider, within the bound.
A program may use at most 128 MiB of HBM per device.

v0:
```python
import jax
import jax.numpy as jnp
from jax import lax
from jax.sharding import PartitionSpec as P

gelu_coef = 0.7978845608028654


def gelu_parts(hidden):
    inner_arg = gelu_coef * (hidden + 0.044715 * hidden * hidden * hidden)
    tangent = jnp.tanh(inner_arg)
    activation = 0.5 * hidden * (1.0 + tangent)
    slope = 0.5 * (1.0 + tangent) + 0.5 * hidden * (1.0 - tangent * tangent) * gelu_coef * (
        1.0 + 3.0 * 0.044715 * hidden * hidden
    )
    return (activation, slope)


def shards(tokens_in, out_grad, w_in, w_out, chosen, counts, gates):
    group_count = lax.axis_size("group")
    exp_local = w_in.shape[0]
    slot_count = chosen.shape[2]
    model_width = tokens_in.shape[1]
    slot_rows = chosen[0].reshape(-1)
    slot_iota = lax.broadcasted_iota(jnp.int32, chosen.shape[1:], 1)
    live_gate = jnp.where(slot_iota < counts[0][:, None], gates[0], jnp.float32(0.0))
    block_shape = (group_count, exp_local, slot_count, model_width)
    picked_x = jnp.take(tokens_in, slot_rows, axis=0).reshape(block_shape)
    picked_grad = (
        (live_gate.reshape(-1)[:, None] * jnp.take(out_grad, slot_rows, axis=0).astype(jnp.float32))
        .astype(jnp.bfloat16)
        .reshape(block_shape)
    )
    near_x, near_grad = (
        lax.all_to_all(picked_x, "group", split_axis=0, concat_axis=0, tiled=True),
        lax.all_to_all(picked_grad, "group", split_axis=0, concat_axis=0, tiled=True),
    )
    rows_x, rows_grad = (
        lax.all_gather(near_x, "fsdp", axis=0, tiled=True),
        lax.all_gather(near_grad, "fsdp", axis=0, tiled=True),
    )
    sources = rows_x.shape[0]
    expert_x = rows_x[:, 0].reshape(-1, model_width)
    expert_grad = rows_grad[:, 0].reshape(-1, model_width)
    hidden = jnp.dot(expert_x, w_in[0], preferred_element_type=jnp.float32)
    activation, gelu_slope = gelu_parts(hidden)
    activation = activation.astype(jnp.bfloat16)
    back_hidden = lax.dot_general(
        expert_grad, w_out[0], (((1,), (1,)), ((), ())), preferred_element_type=jnp.float32
    )
    hidden_grad = (back_hidden * gelu_slope).astype(jnp.bfloat16)
    grads_in_w = [
        lax.dot_general(
            expert_x, hidden_grad, (((0,), (0,)), ((), ())), preferred_element_type=jnp.float32
        )
    ]
    grads_out_w = [
        lax.dot_general(
            activation, expert_grad, (((0,), (0,)), ((), ())), preferred_element_type=jnp.float32
        )
    ]
    hidden_grads = [hidden_grad.reshape(sources, slot_count, -1)]
    stacked_grad = jnp.stack(hidden_grads, axis=1)
    term = jnp.einsum("secf,edf->secd", stacked_grad, w_in, preferred_element_type=jnp.float32)
    partial_grad = term.reshape(sources * exp_local * slot_count, model_width)
    shares = lax.psum_scatter(partial_grad, "fsdp", scatter_dimension=0, tiled=True)
    summed = lax.all_to_all(
        shares.reshape(group_count, exp_local, slot_count, model_width),
        "group",
        split_axis=0,
        concat_axis=0,
        tiled=True,
    )
    grad_tokens = (
        jnp.zeros((tokens_in.shape[0], model_width), jnp.float32)
        .at[slot_rows]
        .add(summed.reshape(-1, model_width))
    )
    return (
        grad_tokens.astype(jnp.bfloat16),
        jnp.stack(grads_in_w, axis=0),
        jnp.stack(grads_out_w, axis=0),
    )


def solution(mesh):
    placed = (
        P(("group", "fsdp"), None),
        P(("group", "fsdp"), None),
        P("group", None, "fsdp"),
        P("group", "fsdp", None),
        P(("group", "fsdp"), None, None),
        P(("group", "fsdp"), None),
        P(("group", "fsdp"), None, None),
    )
    return jax.shard_map(
        shards,
        mesh=mesh,
        in_specs=placed,
        out_specs=(P(("group", "fsdp"), None), P("group", None, "fsdp"), P("group", "fsdp", None)),
        check_vma=False,
    )
```

profile of v0, /device:TPU:1, one launch (start us, length us, event | category | flops | bytes accessed | tf_op | source)
XLA Modules:
  0.0 404.0 jit_solution(8017003688771159239)
XLA Ops:
  7.2 0.0 copy-start
  7.2 0.0 all-gather.5.cloned.1.call-start
  7.2 0.9 reshape_squeeze.12
  8.2 4.2 %gather_fusion.1 = bf16[128,2048]{1,0:T(8,128)(2,1)S(1)} fusion(bf16[1024,2048]{1,0:T(8,128)(2,1)} %param.9, s32[1024]{0:T(1024)S(1)} %pad_clamp_fusion), kind=kCustom, calls=%fused_computation.1.clone | custom fusion | bytes 1049088 | tf_op jit(solution)/shard_map/jit(_take)/gather | solution.py:28
  12.4 0.1 broadcast_select_fusion
  12.5 18.1 %all_to_all.15 = bf16[8,1,16,2048]{3,2,1,0:T(8,128)(2,1)} all-to-all(bf16[8,1,16,2048]{3,2,1,0:T(8,128)(2,1)S(1)} %bitcast.43), channel_id=1, replica_groups=mesh['group'=8,'fsdp'=16] {'group'}, dimensions={0} | all-to-all | bytes 1048576 | tf_op jit(solution)/shard_map/all_to_all | solution.py:35
  30.6 0.0 all-gather.5.cloned.1.call-update
  30.6 0.0 all-gather.3.cloned.1.call-start
  30.7 0.1 squeeze.9
  30.8 0.1 iota_compare_fusion
  30.8 0.1 lt.41
  30.9 4.2 %gather_fusion = bf16[128,2048]{1,0:T(8,128)(2,1)S(1)} fusion(bf16[1024,2048]{1,0:T(8,128)(2,1)} %param.10, s32[1024]{0:T(1024)S(1)} %pad_clamp_fusion), kind=kCustom, calls=%fused_computation.clone | custom fusion | bytes 1049088 | tf_op jit(solution)/shard_map/jit(_take)/gather | solution.py:30
  35.1 0.3 multiply_convert_fusion.2
  35.4 13.5 %all_to_all.16 = bf16[8,1,16,2048]{3,2,1,0:T(8,128)(2,1)} all-to-all(bf16[8,1,16,2048]{3,2,1,0:T(8,128)(2,1)S(1)} %bitcast.42), channel_id=1, replica_groups=mesh['group'=8,'fsdp'=16] {'group'}, dimensions={0} | all-to-all | bytes 1048576 | tf_op jit(solution)/shard_map/all_to_all | solution.py:36
  49.0 0.0 all-gather.3.cloned.1.call-update
  49.0 0.0 reduce-scatter.2.cloned.1.call-start
  49.0 38.3 %all-gather.5.cloned.1.call-done = bf16[128,1,16,2048]{3,2,1,0:T(8,128)(2,1)} async-done(((bf16[8,1,16,2048]{3,2,1,0:T(8,128)(2,1)}), bf16[128,1,16,2048]{3,2,1,0:T(8,128)(2,1)}) %all-gather.5.cloned.1.call-update) | async-done | bytes 8388624 | tf_op jit(solution)/shard_map/all_gather | solution.py:39
  87.3 9.4 %fusion.10 = f32[2048,512]{1,0:T(8,128)} fusion(bf16[2048,2048]{1,0:T(8,128)(2,1)} %bitcast.46, bf16[1,2048,512]{2,1,0:T(8,128)(2,1)S(1)} %copy-done), kind=kOutput, calls=%fused_computation.19 | convolution fusion | flops 4294967296 | bytes 14680064 | tf_op jit(solution)/shard_map/dot_general | solution.py:45
  96.8 46.0 %all-gather.3.cloned.1.call-done = bf16[128,1,16,2048]{3,2,1,0:T(8,128)(2,1)} async-done(((bf16[8,1,16,2048]{3,2,1,0:T(8,128)(2,1)}), bf16[128,1,16,2048]{3,2,1,0:T(8,128)(2,1)}) %all-gather.3.cloned.1.call-update) | async-done | bytes 8388624 | tf_op jit(solution)/shard_map/all_gather | solution.py:40
  142.7 12.1 %fusion.6 = bf16[2048,512]{1,0:T(8,128)(2,1)S(1)} fusion(f32[2048,512]{1,0:T(8,128)} %fusion.10, bf16[2048,2048]{1,0:T(8,128)(2,1)} %bitcast.48, bf16[1,512,2048]{2,1,0:T(8,128)(2,1)} %param.12), kind=kOutput, calls=%fused_computation.12 | convolution fusion | flops 4314890240 | bytes 16777216 | tf_op jit(solution)/shard_map/dot_general | solution.py:48
  154.8 6.3 %convolution_bitcast_fusion = f32[128,1,16,2048]{3,0,2,1:T(8,128)S(1)} fusion(bf16[1,2048,512]{2,1,0:T(8,128)(2,1)S(1)} %copy-done, bf16[128,16,512]{2,1,0:T(8,128)(2,1)S(1)} %bitcast.51), kind=kOutput, calls=%fused_computation.3 | convolution fusion | flops 4294967296 | bytes 20971520 | tf_op jit(solution)/shard_map/secf,edf->secd/dot_general | solution.py:64
  161.2 19.4 %copy.16 = f32[128,1,16,2048]{3,2,0,1:T(8,128)} copy(f32[128,1,16,2048]{3,0,2,1:T(8,128)S(1)} %convolution_bitcast_fusion) | data formatting | bytes 33554432 | tf_op jit(solution)/shard_map/secf,edf->secd/transpose | solution.py:64
  180.6 0.0 reduce-scatter.2.cloned.1.call-update
  180.6 0.7 copy-done.2
  181.3 0.1 reshape_squeeze.11
  181.4 10.5 %convolution_bitcast_fusion.2 = f32[1,2048,512]{2,1,0:T(8,128)} fusion(bf16[2048,2048]{1,0:T(8,128)(2,1)} %bitcast.47, bf16[2048,512]{1,0:T(8,128)(2,1)} %copy-done.5), kind=kOutput, calls=%fused_computation.17 | convolution fusion | flops 4294967296 | bytes 14680064 | tf_op jit(solution)/shard_map/dot_general | solution.py:53
  191.9 170.1 %reduce-scatter.2.cloned.1.call-done = f32[128,2048]{1,0:T(8,128)} async-done(((f32[2048,2048]{1,0:T(8,128)}), f32[128,2048]{1,0:T(8,128)}) %reduce-scatter.2.cloned.1.call-update) | async-done | bytes 1048592 | tf_op jit(solution)/shard_map/reduce_scatter | solution.py:66
  362.0 6.1 %all-to-all-start.2 = ((f32[8,1,16,2048]{3,2,1,0:T(8,128)}), f32[8,1,16,2048]{3,2,1,0:T(8,128)S(1)}, u32[]{:S(2)}, u32[]{:S(2)}) async-start(f32[8,1,16,2048]{3,2,1,0:T(8,128)} %bitcast.44), calls=%async_computation.3 | async-start | bytes 2097152 | tf_op jit(solution)/shard_map/all_to_all | solution.py:67
  368.2 11.5 %convolution_bitcast_fusion.1 = f32[1,512,2048]{2,1,0:T(8,128)} fusion(bf16[2048,2048]{1,0:T(8,128)(2,1)} %bitcast.49, f32[2048,512]{1,0:T(8,128)} %fusion.10), kind=kOutput, calls=%fused_computation.16 | convolution fusion | flops 4304404480 | bytes 16777216 | tf_op jit(solution)/shard_map/dot_general | solution.py:58
  379.7 5.8 %all-to-all-done.2 = f32[8,1,16,2048]{3,2,1,0:T(8,128)S(1)} async-done(((f32[8,1,16,2048]{3,2,1,0:T(8,128)}), f32[8,1,16,2048]{3,2,1,0:T(8,128)S(1)}, u32[]{:S(2)}, u32[]{:S(2)}) %all-to-all-start.2) | async-done | bytes 1048608 | tf_op jit(solution)/shard_map/all_to_all | solution.py:67
  385.6 5.8 %scatter_custom_fusion = f32[1024,2048]{1,0:T(8,128)} fusion(s32[128]{0:T(128)S(1)} %fusion.18, f32[128,2048]{1,0:T(8,128)S(1)} %bitcast.45, f32[]{:T(128)} %constant.0.clone.1), kind=kCustom, calls=%fused_computation.14 | custom fusion | flops 262144 | bytes 8388612 | tf_op jit(solution)/shard_map/scatter-add | solution.py:77
  391.4 6.0 %convert_element_type.18 = bf16[1024,2048]{1,0:T(8,128)(2,1)} convert(f32[1024,2048]{1,0:T(8,128)} %scatter_custom_fusion) | non-fusion elementwise | flops 2097152 | bytes 12582912 | tf_op jit(solution)/shard_map/convert_element_type | solution.py:80
  (15 shorter events, 0.1 us)
Async XLA Ops:
  7.2 80.2 %copy-start = (bf16[1,2048,512]{2,1,0:T(8,128)(2,1)S(1)}, bf16[1,2048,512]{2,1,0:T(8,128)(2,1)}, u32[]{:S(2)}) copy-start(bf16[1,2048,512]{2,1,0:T(8,128)(2,1)} %param.11) | copy-start | bytes 6291460
  7.2 23.5 %copy-start.3 = (f32[1,8,16]{2,1,0:T(8,128)S(1)}, f32[1,8,16]{2,1,0:T(8,128)}, u32[]{:S(2)}) copy-start(f32[1,8,16]{2,1,0:T(8,128)} %param.15) | copy-start | bytes 1540
  7.2 23.6 %copy-start.4 = (s32[1,8]{1,0:T(1,128)S(1)}, s32[1,8]{1,0:T(1,128)}, u32[]{:S(2)}) copy-start(s32[1,8]{1,0:T(1,128)} %param.14) | copy-start | bytes 100
  7.2 80.1 %all-gather.5.cloned.1.call-start = ((), (), s32[]{:S(2)}) async-start(), calls=%async_computation.5 | async-start | bytes 8912896 | tf_op jit(solution)/shard_map/all_gather | solution.py:39
  30.6 112.1 %all-gather.3.cloned.1.call-start = ((), (), s32[]{:S(2)}) async-start(), calls=%async_computation.4 | async-start | bytes 8912896 | tf_op jit(solution)/shard_map/all_gather | solution.py:40
  49.0 313.1 %reduce-scatter.2.cloned.1.call-start = ((), (), s32[]{:S(2)}) async-start(), calls=%async_computation.6 | async-start | bytes 17825792 | tf_op jit(solution)/shard_map/reduce_scatter | solution.py:66
  154.8 6.3 %copy-start.5 = (bf16[2048,512]{1,0:T(8,128)(2,1)}, bf16[2048,512]{1,0:T(8,128)(2,1)S(1)}, u32[]{:S(2)}) copy-start(bf16[2048,512]{1,0:T(8,128)(2,1)S(1)} %fusion.6) | copy-start | bytes 6291460
  180.6 0.7 copy-start.2
  362.0 23.5 %all-to-all-start.2 = ((f32[8,1,16,2048]{3,2,1,0:T(8,128)}), f32[8,1,16,2048]{3,2,1,0:T(8,128)S(1)}, u32[]{:S(2)}, u32[]{:S(2)}) async-start(f32[8,1,16,2048]{3,2,1,0:T(8,128)} %bitcast.44), calls=%async_computation.3 | async-start | bytes 2097152 | tf_op jit(solution)/shard_map/all_to_all | solution.py:67
  385.6 11.9 %copy-start.1 = (bf16[1,2048,512]{2,1,0:T(8,128)(2,1)S(1)}, bf16[1,2048,512]{2,1,0:T(8,128)(2,1)}, u32[]{:S(2)}) copy-start(bf16[1,2048,512]{2,1,0:T(8,128)(2,1)} %param.11) | copy-start | bytes 6291460
Sparse Core Ops, SparseCore 0:
  30.7 56.5 all-gather.4
  89.0 53.6 all-gather.2
  180.7 181.2 reduce-scatter.1
where the time goes:
time: 404 us
  waiting for transfers between devices  260 us (64%)
  matrix products  49.9 us (12%)
  blocking collectives  31.6 us (8%)
  local copies, waits for them, and re-layouts  29.6 us (7%)
  between operations  13.9 us (3%)
  other arithmetic  12.4 us (3%)
  starting transfers between devices  6.26 us (2%)
    reduce_scatter x1, waiting for transfers between devices, shards(): lax.psum_scatter(partial_grad, 'fsdp', scatter_dimension=0, tiled=True)  170 us
    all_gather x1, waiting for transfers between devices, shards(): lax.all_gather(near_grad, 'fsdp', axis=0, tiled=True)  46 us
    all_gather x1, waiting for transfers between devices, shards(): lax.all_gather(near_x, 'fsdp', axis=0, tiled=True)  38.3 us
    transpose x1, local copies, waits for them, and re-layouts, shards(): jnp.einsum('secf,edf->secd', stacked_grad, w_in, preferred_element_type=j...  19.4 us
    all_to_all x1, blocking collectives, shards(): lax.all_to_all(picked_x, 'group', split_axis=0, concat_axis=0, tiled=True)  18.1 us
    all_to_all x1, blocking collectives, shards(): lax.all_to_all(picked_grad, 'group', split_axis=0, concat_axis=0, tiled=T...  13.5 us
    dot_general x1, matrix products, shards(): lax.dot_general(expert_grad, w_out[0], (((1,), (1,)), ((), ())), preferre...  12.1 us
    dot_general x1, matrix products, shards(): lax.dot_general(activation, expert_grad, (((0,), (0,)), ((), ())), prefer...  11.5 us
  transfers between devices with their start and end apart: 4, of which 4 were waited for; matrix products, arithmetic and copies ran while one was open for 9% of the time, Pallas kernels for 0%

commit v1 on v0

--- a/solution.py
+++ b/solution.py
@@ -35,8 +35,17 @@
         lax.all_to_all(picked_x, "group", split_axis=0, concat_axis=0, tiled=True),
         lax.all_to_all(picked_grad, "group", split_axis=0, concat_axis=0, tiled=True),
     )
+
+    def _raise_panels(row_data):
+        return jnp.concatenate(
+            lax.all_to_all(
+                jnp.stack([row_data for _ in range(lax.psum(1, "fsdp"))], 0), "fsdp", 0, 0
+            ),
+            0,
+        )
+
     rows_x, rows_grad = (
-        lax.all_gather(near_x, "fsdp", axis=0, tiled=True),
+        _raise_panels(near_x),
         lax.all_gather(near_grad, "fsdp", axis=0, tiled=True),
     )
     sources = rows_x.shape[0]

time: 404 us -> 450 us (1.11)
  blocking collectives: 31.6 us -> 161 us
  waiting for transfers between devices: 260 us -> 174 us
  local copies, waits for them, and re-layouts: 29.6 us -> 34.6 us
    all_to_all x0 -> x1, blocking collectives: none -> 130 us  [_raise_panels(): lax.all_to_all(jnp.stack([row_data for _ in range(lax.psum(1, 'fsdp'))],...]
    all_gather x1, waiting for transfers between devices: 46 us -> 0.01 us  [shards(): lax.all_gather(near_grad, 'fsdp', axis=0, tiled=True)]
    all_gather x1 -> x0, waiting for transfers between devices: 38.3 us -> none  [shards(): lax.all_gather(near_x, 'fsdp', axis=0, tiled=True)]
    all_to_all x1, blocking collectives: 18.1 us -> 12.9 us  [shards(): lax.all_to_all(picked_x, 'group', split_axis=0, concat_axis=0, tiled=True)]
    all_to_all x1, blocking collectives: 13.5 us -> 18.1 us  [shards(): lax.all_to_all(picked_grad, 'group', split_axis=0, concat_axis=0, tiled=T...]
  transfers between devices with their start and end apart: 4 -> 3, of which waited for: 4 -> 2; matrix products, arithmetic and copies ran while one was open for 9% -> 7% of each run, Pallas kernels for 0% -> 0%
where the time goes in v1:
time: 450 us
  waiting for transfers between devices  174 us (39%)
  blocking collectives  161 us (36%)
  matrix products  46.4 us (10%)
  local copies, waits for them, and re-layouts  34.6 us (8%)
  between operations  14.1 us (3%)
  other arithmetic  13.1 us (3%)
  starting transfers between devices  6.22 us (1%)
    reduce_scatter x1, waiting for transfers between devices, shards(): lax.psum_scatter(partial_grad, 'fsdp', scatter_dimension=0, tiled=True)  169 us
    all_to_all x1, blocking collectives, _raise_panels(): lax.all_to_all(jnp.stack([row_data for _ in range(lax.psum(1, 'fsdp'))],...  130 us
    transpose x1, local copies, waits for them, and re-layouts, shards(): jnp.einsum('secf,edf->secd', stacked_grad, w_in, preferred_element_type=j...  19.4 us
    all_to_all x1, blocking collectives, shards(): lax.all_to_all(picked_grad, 'group', split_axis=0, concat_axis=0, tiled=T...  18.1 us
    all_to_all x1, blocking collectives, shards(): lax.all_to_all(picked_x, 'group', split_axis=0, concat_axis=0, tiled=True)  12.9 us
    dot_general x1, matrix products, shards(): lax.dot_general(expert_grad, w_out[0], (((1,), (1,)), ((), ())), preferre...  12.1 us
    dot_general x1, matrix products, shards(): lax.dot_general(activation, expert_grad, (((0,), (0,)), ((), ())), prefer...  11.5 us
    dot_general x1, matrix products, shards(): lax.dot_general(expert_x, hidden_grad, (((0,), (0,)), ((), ())), preferre...  10.6 us
  transfers between devices with their start and end apart: 3, of which 2 were waited for; matrix products, arithmetic and copies ran while one was open for 7% of the time, Pallas kernels for 0%

profile of v1, /device:TPU:1, one launch (start us, length us, event | category | flops | bytes accessed | tf_op | source)
XLA Modules:
  0.0 449.5 jit_solution(3019836448391505547)
XLA Ops:
  7.2 0.0 copy-start
  7.2 0.0 all-gather.2.cloned.1.call-start
  7.2 0.9 reshape_squeeze.9
  8.2 0.8 squeeze.9
  8.9 0.7 iota_compare_fusion
  9.7 0.1 lt.41
  9.8 4.2 gather_fusion
  13.9 0.3 multiply_convert_fusion.2
  14.2 18.1 %all_to_all.23 = bf16[8,1,16,2048]{3,2,1,0:T(8,128)(2,1)} all-to-all(bf16[8,1,16,2048]{3,2,1,0:T(8,128)(2,1)S(1)} %bitcast.46), channel_id=1, replica_groups=mesh['group'=8,'fsdp'=16] {'group'}, dimensions={0} | all-to-all | bytes 1048576 | tf_op jit(solution)/shard_map/all_to_all | solution.py:36
  32.3 0.0 all-gather.2.cloned.1.call-update
  32.4 0.0 reduce-scatter.2.cloned.1.call-start
  32.4 4.2 gather_fusion.1
  36.6 0.1 broadcast_select_fusion
  36.7 12.9 %all_to_all.24 = bf16[8,1,16,2048]{3,2,1,0:T(8,128)(2,1)S(1)} all-to-all(bf16[8,1,16,2048]{3,2,1,0:T(8,128)(2,1)S(1)} %bitcast.47), channel_id=1, replica_groups=mesh['group'=8,'fsdp'=16] {'group'}, dimensions={0} | all-to-all | bytes 1048576 | tf_op jit(solution)/shard_map/all_to_all | solution.py:35
  49.6 1.1 stack.6
  50.7 129.6 %all_to_all.25 = bf16[16,8,1,16,2048]{4,3,2,1,0:T(8,128)(2,1)S(1)} all-to-all(bf16[16,8,1,16,2048]{4,3,2,1,0:T(8,128)(2,1)S(1)} %stack.6), channel_id=1, replica_groups=mesh['group'=8,'fsdp'=16] {'fsdp'}, dimensions={0} | all-to-all | bytes 16777216 | tf_op jit(solution)/shard_map/all_to_all | solution.py:41
  180.3 3.2 copy-done.2
  183.5 6.0 %fusion.10 = f32[2048,512]{1,0:T(8,128)} fusion(bf16[2048,2048]{1,0:T(8,128)(2,1)S(1)} %bitcast.43, bf16[1,2048,512]{2,1,0:T(8,128)(2,1)S(1)} %copy-done), kind=kOutput, calls=%fused_computation.19 | convolution fusion | flops 4294967296 | bytes 14680064 | tf_op jit(solution)/shard_map/dot_general | solution.py:54
  189.5 12.1 %fusion.6 = bf16[2048,512]{1,0:T(8,128)(2,1)S(1)} fusion(f32[2048,512]{1,0:T(8,128)} %fusion.10, bf16[2048,2048]{1,0:T(8,128)(2,1)} %bitcast.50, bf16[1,512,2048]{2,1,0:T(8,128)(2,1)} %param.12), kind=kOutput, calls=%fused_computation.12 | convolution fusion | flops 4314890240 | bytes 16777216 | tf_op jit(solution)/shard_map/dot_general | solution.py:57
  201.6 0.0 copy-start.4
  201.6 6.3 %convolution_bitcast_fusion = f32[128,1,16,2048]{3,0,2,1:T(8,128)S(1)} fusion(bf16[1,2048,512]{2,1,0:T(8,128)(2,1)S(1)} %copy-done, bf16[128,16,512]{2,1,0:T(8,128)(2,1)S(1)} %bitcast.53), kind=kOutput, calls=%fused_computation.3 | convolution fusion | flops 4294967296 | bytes 20971520 | tf_op jit(solution)/shard_map/secf,edf->secd/dot_general | solution.py:73
  207.9 19.4 %copy.16 = f32[128,1,16,2048]{3,2,0,1:T(8,128)} copy(f32[128,1,16,2048]{3,0,2,1:T(8,128)S(1)} %convolution_bitcast_fusion) | data formatting | bytes 33554432 | tf_op jit(solution)/shard_map/secf,edf->secd/transpose | solution.py:73
  227.3 0.0 reduce-scatter.2.cloned.1.call-update
  227.4 0.7 copy-done.3
  228.0 0.1 reshape_squeeze.8
  228.1 10.6 %convolution_bitcast_fusion.2 = f32[1,2048,512]{2,1,0:T(8,128)} fusion(bf16[2048,2048]{1,0:T(8,128)(2,1)} %bitcast.44, bf16[2048,512]{1,0:T(8,128)(2,1)} %copy-done.4), kind=kOutput, calls=%fused_computation.17 | convolution fusion | flops 4294967296 | bytes 14680064 | tf_op jit(solution)/shard_map/dot_general | solution.py:62
  238.7 168.6 %reduce-scatter.2.cloned.1.call-done = f32[128,2048]{1,0:T(8,128)} async-done(((f32[2048,2048]{1,0:T(8,128)}), f32[128,2048]{1,0:T(8,128)}) %reduce-scatter.2.cloned.1.call-update) | async-done | bytes 1048592 | tf_op jit(solution)/shard_map/reduce_scatter | solution.py:75
  407.2 6.1 %all-to-all-start.3 = ((f32[8,1,16,2048]{3,2,1,0:T(8,128)}), f32[8,1,16,2048]{3,2,1,0:T(8,128)S(1)}, u32[]{:S(2)}, u32[]{:S(2)}) async-start(f32[8,1,16,2048]{3,2,1,0:T(8,128)} %bitcast.48), calls=%async_computation.4 | async-start | bytes 2097152 | tf_op jit(solution)/shard_map/all_to_all | solution.py:76
  413.4 11.5 %convolution_bitcast_fusion.1 = f32[1,512,2048]{2,1,0:T(8,128)} fusion(bf16[2048,2048]{1,0:T(8,128)(2,1)} %bitcast.51, f32[2048,512]{1,0:T(8,128)} %fusion.10), kind=kOutput, calls=%fused_computation.16 | convolution fusion | flops 4304404480 | bytes 16777216 | tf_op jit(solution)/shard_map/dot_general | solution.py:67
  424.9 5.8 %all-to-all-done.3 = f32[8,1,16,2048]{3,2,1,0:T(8,128)S(1)} async-done(((f32[8,1,16,2048]{3,2,1,0:T(8,128)}), f32[8,1,16,2048]{3,2,1,0:T(8,128)S(1)}, u32[]{:S(2)}, u32[]{:S(2)}) %all-to-all-start.3) | async-done | bytes 1048608 | tf_op jit(solution)/shard_map/all_to_all | solution.py:76
  430.8 5.9 %scatter_custom_fusion = f32[1024,2048]{1,0:T(8,128)} fusion(s32[128]{0:T(128)S(1)} %fusion.18, f32[128,2048]{1,0:T(8,128)S(1)} %bitcast.49, f32[]{:T(128)} %constant.0.clone.1), kind=kCustom, calls=%fused_computation.14 | custom fusion | flops 262144 | bytes 8388612 | tf_op jit(solution)/shard_map/scatter-add | solution.py:86
  436.6 6.0 %convert_element_type.18 = bf16[1024,2048]{1,0:T(8,128)(2,1)} convert(f32[1024,2048]{1,0:T(8,128)} %scatter_custom_fusion) | non-fusion elementwise | flops 2097152 | bytes 12582912 | tf_op jit(solution)/shard_map/convert_element_type | solution.py:89
  (12 shorter events, 0.0 us)
Async XLA Ops:
  7.2 176.3 %copy-start = (bf16[1,2048,512]{2,1,0:T(8,128)(2,1)S(1)}, bf16[1,2048,512]{2,1,0:T(8,128)(2,1)}, u32[]{:S(2)}) copy-start(bf16[1,2048,512]{2,1,0:T(8,128)(2,1)} %param.11) | copy-start | bytes 6291460
  7.2 182.3 %all-gather.2.cloned.1.call-start = ((), (), s32[]{:S(2)}) async-start(), calls=%async_computation.5 | async-start | bytes 8912896 | tf_op jit(solution)/shard_map/all_gather | solution.py:49
  32.4 374.9 %reduce-scatter.2.cloned.1.call-start = ((), (), s32[]{:S(2)}) async-start(), calls=%async_computation.6 | async-start | bytes 17825792 | tf_op jit(solution)/shard_map/reduce_scatter | solution.py:75
  180.3 3.2 copy-start.2
  201.6 6.3 %copy-start.4 = (bf16[2048,512]{1,0:T(8,128)(2,1)}, bf16[2048,512]{1,0:T(8,128)(2,1)S(1)}, u32[]{:S(2)}) copy-start(bf16[2048,512]{1,0:T(8,128)(2,1)S(1)} %fusion.6) | copy-start | bytes 6291460
  227.3 0.7 copy-start.3
  407.2 23.5 %all-to-all-start.3 = ((f32[8,1,16,2048]{3,2,1,0:T(8,128)}), f32[8,1,16,2048]{3,2,1,0:T(8,128)S(1)}, u32[]{:S(2)}, u32[]{:S(2)}) async-start(f32[8,1,16,2048]{3,2,1,0:T(8,128)} %bitcast.48), calls=%async_computation.4 | async-start | bytes 2097152 | tf_op jit(solution)/shard_map/all_to_all | solution.py:76
  430.7 11.9 %copy-start.1 = (bf16[1,2048,512]{2,1,0:T(8,128)(2,1)S(1)}, bf16[1,2048,512]{2,1,0:T(8,128)(2,1)}, u32[]{:S(2)}) copy-start(bf16[1,2048,512]{2,1,0:T(8,128)(2,1)} %param.11) | copy-start | bytes 6291460
Sparse Core Ops, SparseCore 0:
  32.5 129.9 all-gather.1
  227.5 179.7 reduce-scatter.1
